TPU v7x, 32 devices: a whole 2x2x4 slice. The times are simulated.
32 devices in a mesh: dp: 2 (over x), cluster: 16 (over z, y, core).
Axes of the slice: x: 2, y: 2, z: 4, core: 2. Of those that a mesh axis runs over, the one named last changes fastest.
Arguments:
- queries: bfloat16 [4096, 768], P(('dp', 'cluster')), may hold values from -6 to 6
- shortlist: int32 [4096, 8], P(('dp', 'cluster')), may hold values from 0 to 15, all different within a row; in each aligned block of 128 rows (0 to 127, 128 to 255, ...) at most 128 rows name the same one
- positives: int32 [4096, 8], P(('dp', 'cluster')), may hold values from 0 to 255
- weights: bfloat16 [16, 256, 768], P('cluster'), may hold values from -0.21875 to 0.21875
- first_moment: float32 [16, 256, 768], P('cluster'), may hold values from -24 to 24
- second_moment: float32 [16, 256, 768], P('cluster'), may hold values from 0.5 to 50
Outputs:
- new_weights: bfloat16 [16, 256, 768], P('cluster')
- new_first: float32 [16, 256, 768], P('cluster')
- new_second: float32 [16, 256, 768], P('cluster')
- query_grad: bfloat16 [4096, 768], P(('dp', 'cluster'))
Inputs may be any that keep to these rules, and one draw needn't show every extreme that they name: `shortlist`: each row names 8 different clusters. In the rows of one device no cluster is named by more than 128 rows, a bound that some block reaches of them.
All inputs are finite; a program needn't handle non-finite values.
Results may differ from a plain program's by a relative error of at most 0.0085.
Values may be sent and summed in bfloat16 or wider, within the bound.
No kernel may reach another device: no remote copies, remote signals or barrier semaphores. Data moves between devices by JAX's collectives and lax.ppermute only.
A program may use at most 64 MiB of HBM per device.

v0:
```python
import jax
import jax.numpy as jnp
from jax import lax
from jax.sharding import PartitionSpec as P

beta_one = 0.9
beta_two = 0.999
learn_rate = 0.01
adam_eps = 1e-08
adam_step = 10.0


def adam_update(cluster_weights, first_moment, second_moment, gradient):
    first_new = beta_one * first_moment + (1.0 - beta_one) * gradient
    second_new = beta_two * second_moment + (1.0 - beta_two) * gradient * gradient
    first_hat = first_new / (1.0 - beta_one**adam_step)
    second_hat = second_new / (1.0 - beta_two**adam_step)
    stepped = cluster_weights.astype(jnp.float32) - learn_rate * first_hat / (
        jnp.sqrt(second_hat) + adam_eps
    )
    return (stepped.astype(jnp.bfloat16), first_new, second_new)


def owner_work(arrived_rows, arrived_labels, cluster_rows):
    label_ids = jnp.arange(cluster_rows.shape[0], dtype=jnp.int32)
    scores = lax.dot_general(
        arrived_rows, cluster_rows, (((1,), (1,)), ((), ())), preferred_element_type=jnp.float32
    )
    target = (arrived_labels[:, None] == label_ids[None, :]).astype(jnp.float32)
    coefficient = (jax.nn.sigmoid(scores) - target).astype(jnp.bfloat16)
    gradient = lax.dot_general(
        coefficient, arrived_rows, (((0,), (0,)), ((), ())), preferred_element_type=jnp.float32
    )
    visit_grad = jnp.dot(coefficient, cluster_rows, preferred_element_type=jnp.float32).astype(
        jnp.bfloat16
    )
    return (gradient, visit_grad)


def on_device(queries, shortlist, positives, weights, first_moment, second_moment):
    owners = lax.axis_size("cluster")
    rows_dev, fanout = shortlist.shape
    feature_dim = queries.shape[1]
    capacity = min(rows_dev, 2 * rows_dev * fanout // owners)
    visits = shortlist.reshape(-1)
    labels = positives.reshape(-1)
    onehot = (visits[:, None] == jnp.arange(owners, dtype=jnp.int32)[None, :]).astype(jnp.int32)
    visit_rank = jnp.sum((jnp.cumsum(onehot, axis=0) - onehot) * onehot, axis=1)
    slot_index = visits * capacity + visit_rank
    slot_visit = (
        jnp.full((owners * capacity,), -1, jnp.int32)
        .at[slot_index]
        .set(jnp.arange(visits.shape[0], dtype=jnp.int32))
    )
    filled = slot_visit >= 0
    clamped = jnp.maximum(slot_visit, 0)
    send_rows = jnp.where(filled[:, None], queries[clamped // fanout], jnp.zeros((), queries.dtype))
    send_labels = jnp.where(filled, labels[clamped], -1)
    cluster_rows = weights[0]
    arrived_rows, arrived_labels = (
        lax.all_to_all(
            send_rows.reshape(owners, capacity, feature_dim),
            "cluster",
            split_axis=0,
            concat_axis=0,
            tiled=True,
        ),
        lax.all_to_all(
            send_labels.reshape(owners, capacity),
            "cluster",
            split_axis=0,
            concat_axis=0,
            tiled=True,
        ),
    )
    gradient, visit_grad = owner_work(
        arrived_rows.reshape(-1, feature_dim), arrived_labels.reshape(-1), cluster_rows
    )
    returned = lax.all_to_all(
        visit_grad.reshape(owners, capacity, feature_dim),
        "cluster",
        split_axis=0,
        concat_axis=0,
        tiled=True,
    )
    per_visit = returned.reshape(-1, feature_dim)[slot_index].astype(jnp.float32)
    query_grad = jnp.sum(per_visit.reshape(rows_dev, fanout, feature_dim), axis=1).astype(
        jnp.bfloat16
    )
    summed = lax.psum(gradient.astype(jnp.bfloat16), "dp").astype(jnp.float32)
    new_weights, new_first, new_second = adam_update(
        cluster_rows, first_moment[0], second_moment[0], summed
    )
    return (new_weights[None], new_first[None], new_second[None], query_grad)


def solution(mesh):
    in_specs = (
        P(("dp", "cluster"), None),
        P(("dp", "cluster"), None),
        P(("dp", "cluster"), None),
        P("cluster", None, None),
        P("cluster", None, None),
        P("cluster", None, None),
    )
    out_specs = (
        P("cluster", None, None),
        P("cluster", None, None),
        P("cluster", None, None),
        P(("dp", "cluster"), None),
    )
    return jax.shard_map(
        on_device, mesh=mesh, in_specs=in_specs, out_specs=out_specs, check_vma=False
    )
```

profile of v0, /device:TPU:13, one launch (start us, length us, event | category | flops | bytes accessed | tf_op | source)
XLA Modules:
  0.0 218.1 jit_solution(6871849412178040356)
XLA Ops:
  7.2 0.7 broadcast_multiply_fusion
  7.9 0.8 copy.13
  8.9 0.1 copy.12
  9.0 0.1 mul.63
  9.1 4.5 %reduce-window.6 = s32[16,8,128]{2,1,0:T(8,128)S(1)} reduce-window(s32[16,8,128]{2,1,0:T(8,128)S(1)} %fusion.15, s32[]{:T(128)} %constant.23.clone.1), window={size=1x1x128 pad=0_0x0_0x127_0}, to_apply=%region_0.0 | reduce-window | flops 2080768 | bytes 131076 | tf_op jit(solution)/shard_map/reduce-window
  13.7 0.1 copy.15
  14.1 4.3 %scatter_custom_fusion = s32[2048]{0:T(1024)S(1)} fusion(s32[1024]{0:T(1024)S(1)} %bitcast.72, s32[1024]{0:T(1024)S(1)} %iota.15, s32[]{:T(128)} %constant.20.clone.1), kind=kCustom, calls=%fused_computation.43 | custom fusion | bytes 8196 | tf_op jit(solution)/shard_map/scatter | solution.py:53
  18.4 0.8 copy.17
  19.3 8.6 %gather_fusion.1 = s32[2048]{0:T(1024)S(1)} fusion(s32[1024]{0:T(1024)S(1)} %reshape.88, s32[2048]{0:T(1024)S(1)} %maximum_clamp_fusion), kind=kCustom, calls=%fused_computation.1 | custom fusion | bytes 24576 | tf_op jit(solution)/shard_map/gather | solution.py:58
  27.9 0.6 broadcast_select_fusion.1
  28.5 6.5 %all-to-all-start.1 = ((s32[16,1,128]{2,1,0:T(1,128)}), s32[16,1,128]{2,1,0:T(1,128)S(1)}, u32[]{:S(2)}, u32[]{:S(2)}) async-start(s32[16,1,128]{2,1,0:T(1,128)} %bitcast.9), calls=%async_computation.1 | async-start | bytes 16384 | tf_op jit(solution)/shard_map/all_to_all | solution.py:68
  35.0 9.4 %gather_fusion = bf16[2048,768]{1,0:T(8,128)(2,1)} fusion(bf16[128,768]{1,0:T(8,128)(2,1)S(1)} %copy-done, s32[2048]{0:T(1024)S(1)} %get-tuple-element.9), kind=kCustom, calls=%fused_computation | custom fusion | bytes 6299648 | tf_op jit(solution)/shard_map/gather | solution.py:57
  44.4 2.1 broadcast_select_fusion
  46.5 75.7 %all_to_all.19 = bf16[16,128,768]{2,1,0:T(8,128)(2,1)S(1)} all-to-all(bf16[16,128,768]{2,1,0:T(8,128)(2,1)S(1)} %broadcast_select_fusion), channel_id=1, replica_groups=mesh['dp'=2,'cluster'=16] {'cluster'}, dimensions={0} | all-to-all | bytes 6291456 | tf_op jit(solution)/shard_map/all_to_all | solution.py:61
  122.2 1.7 copy-done.2
  123.9 1.3 fusion.4
  125.3 2.7 %convolution_convert_fusion = bf16[2048,768]{1,0:T(8,128)(2,1)} fusion(bf16[2048,256]{1,0:T(8,128)(2,1)S(1)} %fusion.4, bf16[1,256,768]{2,1,0:T(8,128)(2,1)S(1)} %copy-done.3), kind=kOutput, calls=%fused_computation.4 | convolution fusion | flops 806879232 | bytes 4587520 | tf_op jit(solution)/shard_map/dot_general | solution.py:34
  127.9 5.1 %all-to-all-start.2 = ((bf16[16,128,768]{2,1,0:T(8,128)(2,1)}), bf16[16,128,768]{2,1,0:T(8,128)(2,1)S(1)}, u32[]{:S(2)}, u32[]{:S(2)}) async-start(bf16[16,128,768]{2,1,0:T(8,128)(2,1)} %bitcast.65), calls=%async_computation.2 | async-start | bytes 6291456 | tf_op jit(solution)/shard_map/all_to_all | solution.py:79
  133.1 4.0 %convolution_convert_fusion.1 = bf16[256,768]{1,0:T(8,128)(2,1)} fusion(bf16[2048,256]{1,0:T(8,128)(2,1)} %copy-done.1, bf16[2048,768]{1,0:T(8,128)(2,1)} %bitcast.68), kind=kOutput, calls=%fused_computation.14 | convolution fusion | flops 805502976 | bytes 4587520 | tf_op jit(solution)/shard_map/dot_general | solution.py:31
  137.1 26.4 %all-reduce.2.cloned.1.call-done = bf16[256,768]{1,0:T(8,128)(2,1)} async-done(((bf16[256,768]{1,0:T(8,128)(2,1)}), bf16[256,768]{1,0:T(8,128)(2,1)}) %all-reduce.2.cloned.1.call-update) | async-done | bytes 393232 | tf_op jit(solution)/shard_map/psum | solution.py:90
  163.5 3.4 %fusion.8 = (f32[1,256,768]{2,1,0:T(8,128)}, bf16[1,256,768]{2,1,0:T(8,128)(2,1)}, f32[1,256,768]{2,1,0:T(8,128)}) fusion(bf16[256,768]{1,0:T(8,128)(2,1)} %all-reduce.2.cloned.1.call-done, f32[1,256,768]{2,1,0:T(8,128)} %param.11, f32[1,256,768]{2,1,0:T(8,128)} %param.10, bf16[1,256,768]{2,1,0:T(8,128)(2,1)} %param.9), kind=kLoop, calls=%fused_computation.21 | loop fusion | flops 2949120 | bytes 4325376 | tf_op jit(solution)/shard_map/broadcast_in_dim | solution.py:94
  166.9 36.0 %all-to-all-done.2 = bf16[16,128,768]{2,1,0:T(8,128)(2,1)S(1)} async-done(((bf16[16,128,768]{2,1,0:T(8,128)(2,1)}), bf16[16,128,768]{2,1,0:T(8,128)(2,1)S(1)}, u32[]{:S(2)}, u32[]{:S(2)}) %all-to-all-start.2) | async-done | bytes 3145760 | tf_op jit(solution)/shard_map/all_to_all | solution.py:79
  202.9 5.2 %gather_fusion.2 = bf16[1024,768]{1,0:T(8,128)(2,1)} fusion(bf16[2048,768]{1,0:T(8,128)(2,1)S(1)} %bitcast.64, s32[1024]{0:T(1024)S(1)} %broadcast_clamp_fusion), kind=kCustom, calls=%fused_computation.2 | custom fusion | bytes 3149824 | tf_op jit(solution)/shard_map/gather | solution.py:86
  208.1 3.1 %bitcast_reduce_fusion = bf16[128,768]{1,0:T(8,128)(2,1)} fusion(bf16[1024,768]{1,0:T(8,128)(2,1)} %gather_fusion.2), kind=kLoop, calls=%fused_computation.13 | loop fusion | flops 688128 | bytes 1769472 | tf_op jit(solution)/shard_map/reduce_sum | solution.py:87
  (24 shorter events, 0.7 us)
Async XLA Ops:
  7.2 27.9 %copy-start = (bf16[128,768]{1,0:T(8,128)(2,1)S(1)}, bf16[128,768]{1,0:T(8,128)(2,1)}, u32[]{:S(2)}) copy-start(bf16[128,768]{1,0:T(8,128)(2,1)} %param.6) | copy-start | bytes 589828
  28.5 18.0 %all-to-all-start.1 = ((s32[16,1,128]{2,1,0:T(1,128)}), s32[16,1,128]{2,1,0:T(1,128)S(1)}, u32[]{:S(2)}, u32[]{:S(2)}) async-start(s32[16,1,128]{2,1,0:T(1,128)} %bitcast.9), calls=%async_computation.1 | async-start | bytes 16384 | tf_op jit(solution)/shard_map/all_to_all | solution.py:68
  46.5 77.4 %copy-start.3 = (bf16[1,256,768]{2,1,0:T(8,128)(2,1)S(1)}, bf16[1,256,768]{2,1,0:T(8,128)(2,1)}, u32[]{:S(2)}) copy-start(bf16[1,256,768]{2,1,0:T(8,128)(2,1)} %param.9) | copy-start | bytes 1179652
  122.2 1.7 copy-start.2
  125.3 2.7 %copy-start.1 = (bf16[2048,256]{1,0:T(8,128)(2,1)}, bf16[2048,256]{1,0:T(8,128)(2,1)S(1)}, u32[]{:S(2)}) copy-start(bf16[2048,256]{1,0:T(8,128)(2,1)S(1)} %fusion.4) | copy-start | bytes 3145732
  127.9 75.0 %all-to-all-start.2 = ((bf16[16,128,768]{2,1,0:T(8,128)(2,1)}), bf16[16,128,768]{2,1,0:T(8,128)(2,1)S(1)}, u32[]{:S(2)}, u32[]{:S(2)}) async-start(bf16[16,128,768]{2,1,0:T(8,128)(2,1)} %bitcast.65), calls=%async_computation.2 | async-start | bytes 6291456 | tf_op jit(solution)/shard_map/all_to_all | solution.py:79
  133.0 30.4 %all-reduce.2.cloned.1.call-start = ((), (), s32[]{:S(2)}) async-start(), calls=%async_computation.3 | async-start | bytes 786432 | tf_op jit(solution)/shard_map/psum | solution.py:90
Sparse Core Ops, SparseCore 0:
  137.2 26.2 all-reduce.1
where the time goes:
time: 219 us; the launch traced here: 218 us
  blocking collectives  75.7 us (35%)
  waiting for transfers between devices  62.4 us (28%)
  local copies, waits for them, and re-layouts  31.5 us (14%)
  other arithmetic  14.7 us (7%)
  between operations  14.2 us (6%)
  starting transfers between devices  11.7 us (5%)
  matrix products  7.95 us (4%)
    all_to_all x1, blocking collectives, on_device(): lax.all_to_all(send_rows.reshape(owners, capacity, feature_dim), 'cluster...  75.7 us
    all_to_all x1, waiting for transfers between devices, on_device(): lax.all_to_all(visit_grad.reshape(owners, capacity, feature_dim), 'cluste...  36 us
    psum x1, waiting for transfers between devices, on_device(): summed = lax.psum(gradient.astype(jnp.bfloat16), 'dp').astype(jnp.float32)  26.4 us
    gather x1, local copies, waits for them, and re-layouts, on_device(): queries[clamped // fanout]  9.38 us
    gather x1, local copies, waits for them, and re-layouts, on_device(): send_labels = jnp.where(filled, labels[clamped], -1)  8.58 us
    all_to_all x1, starting transfers between devices, on_device(): lax.all_to_all(send_labels.reshape(owners, capacity), 'cluster', split_ax...  6.52 us
    gather x1, local copies, waits for them, and re-layouts, on_device(): returned.reshape(-1, feature_dim)[slot_index].astype(jnp.float32)  5.21 us
    all_to_all x1, starting transfers between devices, on_device(): lax.all_to_all(visit_grad.reshape(owners, capacity, feature_dim), 'cluste...  5.1 us
  transfers between devices with their start and end apart: 3, of which 2 were waited for; matrix products, arithmetic and copies ran while one was open for 9% of the time, Pallas kernels for 0%

commit v1 on v0

--- a/solution.py
+++ b/solution.py
@@ -8,6 +8,29 @@
 learn_rate = 0.01
 adam_eps = 1e-08
 adam_step = 10.0
+
+
+def split_up(x, dim, peers):
+    shape = x.shape
+    blocks = x.reshape(*shape[:dim], peers, shape[dim] // peers, *shape[dim + 1 :])
+    return jnp.moveaxis(blocks, dim, 0)
+
+
+def in_order(blocks, dim):
+    blocks = jnp.moveaxis(blocks, 0, dim)
+    dims = blocks.shape
+    return blocks.reshape(*dims[:dim], dims[dim] * dims[dim + 1], *dims[dim + 2 :])
+
+
+def exchange_in_pairs(x, axis, split_dim, concat_dim):
+    count, index = (lax.axis_size(axis), lax.axis_index(axis))
+    blocks = split_up(x, split_dim, count)
+    finished = [blocks[index]]
+    for lap in range(1, count):
+        sent = blocks[index ^ lap]
+        finished.append(lax.ppermute(sent, axis, [(i, i ^ lap) for i in range(count)]))
+    blocks = jnp.stack(finished)[index ^ jnp.arange(count)]
+    return in_order(blocks, concat_dim)
 
 
 def adam_update(cluster_weights, first_moment, second_moment, gradient):
@@ -58,13 +81,7 @@
     send_labels = jnp.where(filled, labels[clamped], -1)
     cluster_rows = weights[0]
     arrived_rows, arrived_labels = (
-        lax.all_to_all(
-            send_rows.reshape(owners, capacity, feature_dim),
-            "cluster",
-            split_axis=0,
-            concat_axis=0,
-            tiled=True,
-        ),
+        exchange_in_pairs(send_rows.reshape(owners, capacity, feature_dim), "cluster", 0, 0),
         lax.all_to_all(
             send_labels.reshape(owners, capacity),
             "cluster",

time: 219 us -> 227 us (1.037)
  blocking collectives: 75.7 us -> 0 us
  waiting for transfers between devices: 62.4 us -> 113 us
  starting transfers between devices: 11.7 us -> 30.5 us
  local copies, waits for them, and re-layouts: 31.5 us -> 44.5 us
    all_to_all x1 -> x0, blocking collectives: 75.7 us -> none  [on_device(): lax.all_to_all(send_rows.reshape(owners, capacity, feature_dim), 'cluster...]
    ppermute x0 -> x15, waiting for transfers between devices: none -> 50.4 us  [exchange_in_pairs(): lax.ppermute(sent, axis, [(i, i ^ lap) for i in range(count)])]
    ppermute x0 -> x15, starting transfers between devices: none -> 18.4 us  [exchange_in_pairs(): lax.ppermute(sent, axis, [(i, i ^ lap) for i in range(count)])]
    unnamed x10 -> x26, local copies, waits for them, and re-layouts: 3.3 us -> 11.2 us
    gather x0 -> x1, local copies, waits for them, and re-layouts: none -> 2.64 us  [exchange_in_pairs(): blocks = jnp.stack(finished)[index ^ jnp.arange(count)]]
  transfers between devices with their start and end apart: 3 -> 18, of which waited for: 2 -> 9; matrix products, arithmetic and copies ran while one was open for 9% -> 9% of each run, Pallas kernels for 0% -> 0%
where the time goes in v1:
time: 227 us; the launch traced here: 226 us
  waiting for transfers between devices  113 us (50%)
  local copies, waits for them, and re-layouts  44.5 us (20%)
  starting transfers between devices  30.5 us (13%)
  other arithmetic  14.7 us (6%)
  between operations  14.4 us (6%)
  matrix products  9.35 us (4%)
    ppermute x15, waiting for transfers between devices, exchange_in_pairs(): lax.ppermute(sent, axis, [(i, i ^ lap) for i in range(count)])  50.4 us
    all_to_all x1, waiting for transfers between devices, on_device(): lax.all_to_all(visit_grad.reshape(owners, capacity, feature_dim), 'cluste...  36 us
    psum x1, waiting for transfers between devices, on_device(): summed = lax.psum(gradient.astype(jnp.bfloat16), 'dp').astype(jnp.float32)  26.4 us
    ppermute x15, starting transfers between devices, exchange_in_pairs(): lax.ppermute(sent, axis, [(i, i ^ lap) for i in range(count)])  18.4 us
    unnamed x26, local copies, waits for them, and re-layouts  11.2 us
    gather x1, local copies, waits for them, and re-layouts, on_device(): queries[clamped // fanout]  9.4 us
    gather x1, local copies, waits for them, and re-layouts, on_device(): send_labels = jnp.where(filled, labels[clamped], -1)  8.58 us
    all_to_all x1, starting transfers between devices, on_device(): lax.all_to_all(visit_grad.reshape(owners, capacity, feature_dim), 'cluste...  6.13 us
  transfers between devices with their start and end apart: 18, of which 9 were waited for; matrix products, arithmetic and copies ran while one was open for 9% of the time, Pallas kernels for 0%

profile of v1, /device:TPU:13, one launch (start us, length us, event | category | flops | bytes accessed | tf_op | source)
XLA Modules:
  0.0 226.3 jit_solution(8333428123035422490)
XLA Ops:
  10.0 4.5 %reduce-window.6 = s32[16,8,128]{2,1,0:T(8,128)S(1)} reduce-window(s32[16,8,128]{2,1,0:T(8,128)S(1)} %fusion.15, s32[]{:T(128)} %constant.34.clone.1), window={size=1x1x128 pad=0_0x0_0x127_0}, to_apply=%region_0.0 | reduce-window | flops 2080768 | bytes 131076 | tf_op jit(solution)/shard_map/reduce-window
  15.0 4.3 %scatter_custom_fusion = s32[2048]{0:T(1024)S(1)} fusion(s32[1024]{0:T(1024)S(1)} %bitcast.135, s32[1024]{0:T(1024)S(1)} %iota.19, s32[]{:T(128)} %constant.32.clone.1), kind=kCustom, calls=%fused_computation.76 | custom fusion | bytes 8196 | tf_op jit(solution)/shard_map/scatter | solution.py:76
  19.4 8.6 %gather_fusion.2 = s32[2048]{0:T(1024)S(1)} fusion(s32[1024]{0:T(1024)S(1)} %reshape.110, s32[2048]{0:T(1024)S(1)} %maximum_clamp_fusion), kind=kCustom, calls=%fused_computation.2 | custom fusion | bytes 24576 | tf_op jit(solution)/shard_map/gather | solution.py:81
  28.6 9.4 %gather_fusion = bf16[2048,768]{1,0:T(8,128)(2,1)} fusion(bf16[128,768]{1,0:T(8,128)(2,1)S(1)} %copy-done, s32[2048]{0:T(1024)S(1)} %get-tuple-element.25), kind=kCustom, calls=%fused_computation | custom fusion | bytes 6299648 | tf_op jit(solution)/shard_map/gather | solution.py:80
  46.0 6.0 %all-to-all-start = ((s32[16,1,128]{2,1,0:T(1,128)}), s32[16,1,128]{2,1,0:T(1,128)S(1)}, u32[]{:S(2)}, u32[]{:S(2)}) async-start(s32[16,1,128]{2,1,0:T(1,128)} %bitcast.41), calls=%async_computation | async-start | bytes 16384 | tf_op jit(solution)/shard_map/all_to_all | solution.py:85
  52.9 2.8 %collective-permute-start.6 = (bf16[1,128,768]{2,1,0:T(8,128)(2,1)}, bf16[1,128,768]{2,1,0:T(8,128)(2,1)S(1)}, u32[]{:S(2)}, u32[]{:S(2)}) collective-permute-start(bf16[1,128,768]{2,1,0:T(8,128)(2,1)} %get-tuple-element.14), channel_id=1, source_target_pairs={{0,7},{1,6},{2,5},{3,4},{4,3},{5,2},{6,1},{7,0},{8,15},{9,14},{10,... | collective-permute-start | bytes 589832 | tf_op jit(solution)/shard_map/ppermute | solution.py:31
  62.9 4.9 %collective-permute-start.10 = (bf16[1,128,768]{2,1,0:T(8,128)(2,1)}, bf16[1,128,768]{2,1,0:T(8,128)(2,1)S(1)}, u32[]{:S(2)}, u32[]{:S(2)}) collective-permute-start(bf16[1,128,768]{2,1,0:T(8,128)(2,1)} %get-tuple-element.10), channel_id=1, source_target_pairs={{0,11},{1,10},{2,9},{3,8},{4,15},{5,14},{6,13},{7,12},{8,3},{9,2},... | collective-permute-start | bytes 589832 | tf_op jit(solution)/shard_map/ppermute | solution.py:31
  71.5 19.1 %collective-permute-done.8 = bf16[1,128,768]{2,1,0:T(8,128)(2,1)S(1)} collective-permute-done((bf16[1,128,768]{2,1,0:T(8,128)(2,1)}, bf16[1,128,768]{2,1,0:T(8,128)(2,1)S(1)}, u32[]{:S(2)}, u32[]{:S(2)}) %collective-permute-start.8) | collective-permute-done | bytes 196640 | tf_op jit(solution)/shard_map/ppermute | solution.py:31
  91.3 9.8 %collective-permute-done.9 = bf16[1,128,768]{2,1,0:T(8,128)(2,1)S(1)} collective-permute-done((bf16[1,128,768]{2,1,0:T(8,128)(2,1)}, bf16[1,128,768]{2,1,0:T(8,128)(2,1)S(1)}, u32[]{:S(2)}, u32[]{:S(2)}) %collective-permute-start.9) | collective-permute-done | bytes 196640 | tf_op jit(solution)/shard_map/ppermute | solution.py:31
  102.1 3.3 %collective-permute-done.10 = bf16[1,128,768]{2,1,0:T(8,128)(2,1)S(1)} collective-permute-done((bf16[1,128,768]{2,1,0:T(8,128)(2,1)}, bf16[1,128,768]{2,1,0:T(8,128)(2,1)S(1)}, u32[]{:S(2)}, u32[]{:S(2)}) %collective-permute-start.10) | collective-permute-done | bytes 196640 | tf_op jit(solution)/shard_map/ppermute | solution.py:31
  106.0 7.7 %collective-permute-done.11 = bf16[1,128,768]{2,1,0:T(8,128)(2,1)S(1)} collective-permute-done((bf16[1,128,768]{2,1,0:T(8,128)(2,1)}, bf16[1,128,768]{2,1,0:T(8,128)(2,1)S(1)}, u32[]{:S(2)}, u32[]{:S(2)}) %collective-permute-start.11) | collective-permute-done | bytes 196640 | tf_op jit(solution)/shard_map/ppermute | solution.py:31
  114.5 3.8 %collective-permute-done.12 = bf16[1,128,768]{2,1,0:T(8,128)(2,1)S(1)} collective-permute-done((bf16[1,128,768]{2,1,0:T(8,128)(2,1)}, bf16[1,128,768]{2,1,0:T(8,128)(2,1)S(1)}, u32[]{:S(2)}, u32[]{:S(2)}) %collective-permute-start.12) | collective-permute-done | bytes 196640 | tf_op jit(solution)/shard_map/ppermute | solution.py:31
  119.0 3.1 %collective-permute-done.13 = bf16[1,128,768]{2,1,0:T(8,128)(2,1)S(1)} collective-permute-done((bf16[1,128,768]{2,1,0:T(8,128)(2,1)S(1)}, bf16[1,128,768]{2,1,0:T(8,128)(2,1)S(1)}, u32[]{:S(2)}, u32[]{:S(2)}) %collective-permute-start.13) | collective-permute-done | bytes 196640 | tf_op jit(solution)/shard_map/ppermute | solution.py:31
  122.8 3.5 %collective-permute-done.14 = bf16[1,128,768]{2,1,0:T(8,128)(2,1)S(1)} collective-permute-done((bf16[1,128,768]{2,1,0:T(8,128)(2,1)S(1)}, bf16[1,128,768]{2,1,0:T(8,128)(2,1)S(1)}, u32[]{:S(2)}, u32[]{:S(2)}) %collective-permute-start.14) | collective-permute-done | bytes 196640 | tf_op jit(solution)/shard_map/ppermute | solution.py:31
  127.0 2.6 %gather_fusion.1 = bf16[16,128,768]{2,1,0:T(8,128)(2,1)S(1)} fusion(bf16[16,128,768]{2,1,0:T(8,128)(2,1)} %bitcast.129, s32[1024]{0:T(1024)S(1)} %pad_clamp_fusion), kind=kCustom, calls=%fused_computation.1 | custom fusion | bytes 6291520 | tf_op jit(solution)/shard_map/gather | solution.py:32
  129.7 2.8 %fusion.4 = bf16[2048,256]{1,0:T(8,128)(2,1)S(1)} fusion(bf16[2048,768]{1,0:T(8,128)(2,1)S(1)} %bitcast.130, s32[2048]{0:T(1024)S(1)} %bitcast.138, bf16[1,256,768]{2,1,0:T(8,128)(2,1)} %param.9), kind=kOutput, calls=%fused_computation.12 | convolution fusion | flops 808976384 | bytes 4595712 | tf_op jit(solution)/shard_map/dot_general | solution.py:49
  132.5 2.6 %convolution_convert_fusion = bf16[2048,768]{1,0:T(8,128)(2,1)} fusion(bf16[2048,256]{1,0:T(8,128)(2,1)S(1)} %fusion.4, bf16[1,256,768]{2,1,0:T(8,128)(2,1)S(1)} %copy-done.3), kind=kOutput, calls=%fused_computation.5 | convolution fusion | flops 806879232 | bytes 4587520 | tf_op jit(solution)/shard_map/dot_general | solution.py:57
  135.1 6.1 %all-to-all-start.1 = ((bf16[16,128,768]{2,1,0:T(8,128)(2,1)}), bf16[16,128,768]{2,1,0:T(8,128)(2,1)S(1)}, u32[]{:S(2)}, u32[]{:S(2)}) async-start(bf16[16,128,768]{2,1,0:T(8,128)(2,1)} %bitcast.127), calls=%async_computation.1 | async-start | bytes 6291456 | tf_op jit(solution)/shard_map/all_to_all | solution.py:96
  141.3 4.0 %convolution_convert_fusion.1 = bf16[256,768]{1,0:T(8,128)(2,1)} fusion(bf16[2048,256]{1,0:T(8,128)(2,1)} %copy-done.1, bf16[2048,768]{1,0:T(8,128)(2,1)} %bitcast.131), kind=kOutput, calls=%fused_computation.15 | convolution fusion | flops 805502976 | bytes 4587520 | tf_op jit(solution)/shard_map/dot_general | solution.py:54
  145.3 26.4 %all-reduce.2.cloned.1.call-done = bf16[256,768]{1,0:T(8,128)(2,1)} async-done(((bf16[256,768]{1,0:T(8,128)(2,1)}), bf16[256,768]{1,0:T(8,128)(2,1)}) %all-reduce.2.cloned.1.call-update) | async-done | bytes 393232 | tf_op jit(solution)/shard_map/psum | solution.py:107
  171.7 3.4 %fusion.8 = (f32[1,256,768]{2,1,0:T(8,128)}, bf16[1,256,768]{2,1,0:T(8,128)(2,1)}, f32[1,256,768]{2,1,0:T(8,128)}) fusion(bf16[256,768]{1,0:T(8,128)(2,1)} %all-reduce.2.cloned.1.call-done, f32[1,256,768]{2,1,0:T(8,128)} %param.11, f32[1,256,768]{2,1,0:T(8,128)} %param.10, bf16[1,256,768]{2,1,0:T(8,128)(2,1)} %param.9), kind=kLoop, calls=%fused_computation.22 | loop fusion | flops 2949120 | bytes 4325376 | tf_op jit(solution)/shard_map/broadcast_in_dim | solution.py:111
  175.1 36.0 %all-to-all-done.1 = bf16[16,128,768]{2,1,0:T(8,128)(2,1)S(1)} async-done(((bf16[16,128,768]{2,1,0:T(8,128)(2,1)}), bf16[16,128,768]{2,1,0:T(8,128)(2,1)S(1)}, u32[]{:S(2)}, u32[]{:S(2)}) %all-to-all-start.1) | async-done | bytes 3145760 | tf_op jit(solution)/shard_map/all_to_all | solution.py:96
  211.1 5.2 %gather_fusion.3 = bf16[1024,768]{1,0:T(8,128)(2,1)} fusion(bf16[2048,768]{1,0:T(8,128)(2,1)S(1)} %bitcast.126, s32[1024]{0:T(1024)S(1)} %broadcast_clamp_fusion), kind=kCustom, calls=%fused_computation.3 | custom fusion | bytes 3149824 | tf_op jit(solution)/shard_map/gather | solution.py:103
  216.3 3.1 %bitcast_reduce_fusion = bf16[128,768]{1,0:T(8,128)(2,1)} fusion(bf16[1024,768]{1,0:T(8,128)(2,1)} %gather_fusion.3), kind=kLoop, calls=%fused_computation.14 | loop fusion | flops 688128 | bytes 1769472 | tf_op jit(solution)/shard_map/reduce_sum | solution.py:104
  (74 shorter events, 28.7 us)
Async XLA Ops:
  7.2 21.4 %copy-start = (bf16[128,768]{1,0:T(8,128)(2,1)S(1)}, bf16[128,768]{1,0:T(8,128)(2,1)}, u32[]{:S(2)}) copy-start(bf16[128,768]{1,0:T(8,128)(2,1)} %param.6) | copy-start | bytes 589828
  41.8 48.8 %copy-start.4 = (bf16[1,128,768]{2,1,0:T(8,128)(2,1)S(1)}, bf16[1,128,768]{2,1,0:T(8,128)(2,1)}, u32[]{:S(2)}) copy-start(bf16[1,128,768]{2,1,0:T(8,128)(2,1)} %get-tuple-element.7) | copy-start | bytes 589828
  41.8 10.2 %collective-permute-start = (bf16[1,128,768]{2,1,0:T(8,128)(2,1)}, bf16[1,128,768]{2,1,0:T(8,128)(2,1)S(1)}, u32[]{:S(2)}, u32[]{:S(2)}) collective-permute-start(bf16[1,128,768]{2,1,0:T(8,128)(2,1)} %get-tuple-element.20), channel_id=1, source_target_pairs={{0,1},{1,0},{2,3},{3,2},{4,5},{5,4},{6,7},{7,6},{8,9},{9,8},{10,11... | collective-permute-start | bytes 589832 | tf_op jit(solution)/shard_map/ppermute | solution.py:31
  42.5 10.4 %collective-permute-start.1 = (bf16[1,128,768]{2,1,0:T(8,128)(2,1)}, bf16[1,128,768]{2,1,0:T(8,128)(2,1)S(1)}, u32[]{:S(2)}, u32[]{:S(2)}) collective-permute-start(bf16[1,128,768]{2,1,0:T(8,128)(2,1)} %get-tuple-element.19), channel_id=1, source_target_pairs={{0,2},{1,3},{2,0},{3,1},{4,6},{5,7},{6,4},{7,5},{8,10},{9,11},{10,... | collective-permute-start | bytes 589832 | tf_op jit(solution)/shard_map/ppermute | solution.py:31
  42.7 13.6 %collective-permute-start.2 = (bf16[1,128,768]{2,1,0:T(8,128)(2,1)}, bf16[1,128,768]{2,1,0:T(8,128)(2,1)S(1)}, u32[]{:S(2)}, u32[]{:S(2)}) collective-permute-start(bf16[1,128,768]{2,1,0:T(8,128)(2,1)} %get-tuple-element.18), channel_id=1, source_target_pairs={{0,3},{1,2},{2,1},{3,0},{4,7},{5,6},{6,5},{7,4},{8,11},{9,10},{10,... | collective-permute-start | bytes 589832 | tf_op jit(solution)/shard_map/ppermute | solution.py:31
  44.2 14.9 %collective-permute-start.3 = (bf16[1,128,768]{2,1,0:T(8,128)(2,1)}, bf16[1,128,768]{2,1,0:T(8,128)(2,1)S(1)}, u32[]{:S(2)}, u32[]{:S(2)}) collective-permute-start(bf16[1,128,768]{2,1,0:T(8,128)(2,1)} %get-tuple-element.17), channel_id=1, source_target_pairs={{0,4},{1,5},{2,6},{3,7},{4,0},{5,1},{6,2},{7,3},{8,12},{9,13},{10,... | collective-permute-start | bytes 589832 | tf_op jit(solution)/shard_map/ppermute | solution.py:31
  44.4 15.7 %collective-permute-start.4 = (bf16[1,128,768]{2,1,0:T(8,128)(2,1)}, bf16[1,128,768]{2,1,0:T(8,128)(2,1)S(1)}, u32[]{:S(2)}, u32[]{:S(2)}) collective-permute-start(bf16[1,128,768]{2,1,0:T(8,128)(2,1)} %get-tuple-element.16), channel_id=1, source_target_pairs={{0,5},{1,4},{2,7},{3,6},{4,1},{5,0},{6,3},{7,2},{8,13},{9,12},{10,... | collective-permute-start | bytes 589832 | tf_op jit(solution)/shard_map/ppermute | solution.py:31
  46.0 83.7 %all-to-all-start = ((s32[16,1,128]{2,1,0:T(1,128)}), s32[16,1,128]{2,1,0:T(1,128)S(1)}, u32[]{:S(2)}, u32[]{:S(2)}) async-start(s32[16,1,128]{2,1,0:T(1,128)} %bitcast.41), calls=%async_computation | async-start | bytes 16384 | tf_op jit(solution)/shard_map/all_to_all | solution.py:85
  52.0 10.9 %collective-permute-start.5 = (bf16[1,128,768]{2,1,0:T(8,128)(2,1)}, bf16[1,128,768]{2,1,0:T(8,128)(2,1)S(1)}, u32[]{:S(2)}, u32[]{:S(2)}) collective-permute-start(bf16[1,128,768]{2,1,0:T(8,128)(2,1)} %get-tuple-element.15), channel_id=1, source_target_pairs={{0,6},{1,7},{2,4},{3,5},{4,2},{5,3},{6,0},{7,1},{8,14},{9,15},{10,... | collective-permute-start | bytes 589832 | tf_op jit(solution)/shard_map/ppermute | solution.py:31
  52.9 15.6 %collective-permute-start.6 = (bf16[1,128,768]{2,1,0:T(8,128)(2,1)}, bf16[1,128,768]{2,1,0:T(8,128)(2,1)S(1)}, u32[]{:S(2)}, u32[]{:S(2)}) collective-permute-start(bf16[1,128,768]{2,1,0:T(8,128)(2,1)} %get-tuple-element.14), channel_id=1, source_target_pairs={{0,7},{1,6},{2,5},{3,4},{4,3},{5,2},{6,1},{7,0},{8,15},{9,14},{10,... | collective-permute-start | bytes 589832 | tf_op jit(solution)/shard_map/ppermute | solution.py:31
  56.3 13.4 %collective-permute-start.7 = (bf16[1,128,768]{2,1,0:T(8,128)(2,1)}, bf16[1,128,768]{2,1,0:T(8,128)(2,1)S(1)}, u32[]{:S(2)}, u32[]{:S(2)}) collective-permute-start(bf16[1,128,768]{2,1,0:T(8,128)(2,1)} %get-tuple-element.13), channel_id=1, source_target_pairs={{0,8},{1,9},{2,10},{3,11},{4,12},{5,13},{6,14},{7,15},{8,0},{9,1},... | collective-permute-start | bytes 589832 | tf_op jit(solution)/shard_map/ppermute | solution.py:31
  59.1 31.5 %collective-permute-start.8 = (bf16[1,128,768]{2,1,0:T(8,128)(2,1)}, bf16[1,128,768]{2,1,0:T(8,128)(2,1)S(1)}, u32[]{:S(2)}, u32[]{:S(2)}) collective-permute-start(bf16[1,128,768]{2,1,0:T(8,128)(2,1)} %get-tuple-element.12), channel_id=1, source_target_pairs={{0,9},{1,8},{2,11},{3,10},{4,13},{5,12},{6,15},{7,14},{8,1},{9,0},... | collective-permute-start | bytes 589832 | tf_op jit(solution)/shard_map/ppermute | solution.py:31
  60.1 41.0 %collective-permute-start.9 = (bf16[1,128,768]{2,1,0:T(8,128)(2,1)}, bf16[1,128,768]{2,1,0:T(8,128)(2,1)S(1)}, u32[]{:S(2)}, u32[]{:S(2)}) collective-permute-start(bf16[1,128,768]{2,1,0:T(8,128)(2,1)} %get-tuple-element.11), channel_id=1, source_target_pairs={{0,10},{1,11},{2,8},{3,9},{4,14},{5,15},{6,12},{7,13},{8,2},{9,3},... | collective-permute-start | bytes 589832 | tf_op jit(solution)/shard_map/ppermute | solution.py:31
  62.9 42.5 %collective-permute-start.10 = (bf16[1,128,768]{2,1,0:T(8,128)(2,1)}, bf16[1,128,768]{2,1,0:T(8,128)(2,1)S(1)}, u32[]{:S(2)}, u32[]{:S(2)}) collective-permute-start(bf16[1,128,768]{2,1,0:T(8,128)(2,1)} %get-tuple-element.10), channel_id=1, source_target_pairs={{0,11},{1,10},{2,9},{3,8},{4,15},{5,14},{6,13},{7,12},{8,3},{9,2},... | collective-permute-start | bytes 589832 | tf_op jit(solution)/shard_map/ppermute | solution.py:31
  68.5 45.3 %collective-permute-start.11 = (bf16[1,128,768]{2,1,0:T(8,128)(2,1)}, bf16[1,128,768]{2,1,0:T(8,128)(2,1)S(1)}, u32[]{:S(2)}, u32[]{:S(2)}) collective-permute-start(bf16[1,128,768]{2,1,0:T(8,128)(2,1)} %get-tuple-element.9), channel_id=1, source_target_pairs={{0,12},{1,13},{2,14},{3,15},{4,8},{5,9},{6,10},{7,11},{8,4},{9,5},... | collective-permute-start | bytes 589832 | tf_op jit(solution)/shard_map/ppermute | solution.py:31
  69.8 48.5 %collective-permute-start.12 = (bf16[1,128,768]{2,1,0:T(8,128)(2,1)}, bf16[1,128,768]{2,1,0:T(8,128)(2,1)S(1)}, u32[]{:S(2)}, u32[]{:S(2)}) collective-permute-start(bf16[1,128,768]{2,1,0:T(8,128)(2,1)} %get-tuple-element.8), channel_id=1, source_target_pairs={{0,13},{1,12},{2,15},{3,14},{4,9},{5,8},{6,11},{7,10},{8,5},{9,4},... | collective-permute-start | bytes 589832 | tf_op jit(solution)/shard_map/ppermute | solution.py:31
  90.6 31.5 %collective-permute-start.13 = (bf16[1,128,768]{2,1,0:T(8,128)(2,1)S(1)}, bf16[1,128,768]{2,1,0:T(8,128)(2,1)S(1)}, u32[]{:S(2)}, u32[]{:S(2)}) collective-permute-start(bf16[1,128,768]{2,1,0:T(8,128)(2,1)S(1)} %copy-done.4), channel_id=1, source_target_pairs={{0,14},{1,15},{2,12},{3,13},{4,10},{5,11},{6,8},{7,9},{8,6},{9,7},... | collective-permute-start | bytes 589832 | tf_op jit(solution)/shard_map/ppermute | solution.py:31
  101.1 25.2 %collective-permute-start.14 = (bf16[1,128,768]{2,1,0:T(8,128)(2,1)S(1)}, bf16[1,128,768]{2,1,0:T(8,128)(2,1)S(1)}, u32[]{:S(2)}, u32[]{:S(2)}) collective-permute-start(bf16[1,128,768]{2,1,0:T(8,128)(2,1)S(1)} %get-tuple-element.6), channel_id=1, source_target_pairs={{0,15},{1,14},{2,13},{3,12},{4,11},{5,10},{6,9},{7,8},{8,7},{9,6},... | collective-permute-start | bytes 589832 | tf_op jit(solution)/shard_map/ppermute | solution.py:31
  129.7 2.8 %copy-start.2 = (bf16[16,128,768]{2,1,0:T(8,128)(2,1)}, bf16[16,128,768]{2,1,0:T(8,128)(2,1)S(1)}, u32[]{:S(2)}) copy-start(bf16[16,128,768]{2,1,0:T(8,128)(2,1)S(1)} %gather_fusion.1) | copy-start | bytes 9437188
  129.7 2.8 %copy-start.3 = (bf16[1,256,768]{2,1,0:T(8,128)(2,1)S(1)}, bf16[1,256,768]{2,1,0:T(8,128)(2,1)}, u32[]{:S(2)}) copy-start(bf16[1,256,768]{2,1,0:T(8,128)(2,1)} %param.9) | copy-start | bytes 1179652
  132.5 2.6 %copy-start.1 = (bf16[2048,256]{1,0:T(8,128)(2,1)}, bf16[2048,256]{1,0:T(8,128)(2,1)S(1)}, u32[]{:S(2)}) copy-start(bf16[2048,256]{1,0:T(8,128)(2,1)S(1)} %fusion.4) | copy-start | bytes 3145732
  135.1 76.0 %all-to-all-start.1 = ((bf16[16,128,768]{2,1,0:T(8,128)(2,1)}), bf16[16,128,768]{2,1,0:T(8,128)(2,1)S(1)}, u32[]{:S(2)}, u32[]{:S(2)}) async-start(bf16[16,128,768]{2,1,0:T(8,128)(2,1)} %bitcast.127), calls=%async_computation.1 | async-start | bytes 6291456 | tf_op jit(solution)/shard_map/all_to_all | solution.py:96
  141.2 30.5 %all-reduce.2.cloned.1.call-start = ((), (), s32[]{:S(2)}) async-start(), calls=%async_computation.2 | async-start | bytes 786432 | tf_op jit(solution)/shard_map/psum | solution.py:107
Sparse Core Ops, SparseCore 0:
  145.4 26.2 all-reduce.1
